TPU v7x, 256 devices: a whole 4x4x8 slice. The times are simulated.
256 devices in a mesh: rows: 32 (over z, x), cols: 8 (over y, core).
Axes of the slice: x: 4, y: 4, z: 8, core: 2. Of those that a mesh axis runs over, the one named last changes fastest.
Arguments:
- block_values: bfloat16 [256, 256, 128, 128], P('rows', 'cols')
- block_columns: int32 [256, 256], P('rows', 'cols'), may hold values from 0 to 1023, as said below
- row_counts: int32 [256, 8], P('rows', 'cols'), may hold values from 1 to 32, as said below
- sketch: bfloat16 [1048576, 256], P(('rows', 'cols')), may hold values from -6 to 6
Outputs:
- basis: float32 [32768, 256], P(('rows', 'cols'))
- triangle: float32 [256, 256], replicated
Inputs may be any that keep to these rules, and one draw needn't show every extreme that they name: row_counts[b, c] counts the live slots among slots c * 32 to c * 32 + 31 of block-row b; some entry equals 32. `block_columns`: take the 8 x 32 slots of one index of rows and one column group c; among them at most 12 name block-columns j with the same j // 32, and in every such set some j // 32 is named by exactly 12 slots.
All inputs are finite; a program needn't handle non-finite values.
Results may differ from a plain program's by a relative error of at most 0.0003.
Values may be sent and summed in bfloat16 or wider, within the bound.
No kernel may reach another device: no remote copies, remote signals or barrier semaphores. Data moves between devices by JAX's collectives and lax.ppermute only.
A program may use at most 128 MiB of HBM per device.

v0:
```python
import jax
import jax.numpy as jnp
from jax import lax
from jax.sharding import PartitionSpec as P


def request_table(columns_flat, per_owner, axis_rows, capacity):
    owners = columns_flat // per_owner
    onehot = (owners[:, None] == jnp.arange(axis_rows, dtype=jnp.int32)[None, :]).astype(jnp.int32)
    before = jnp.cumsum(onehot, axis=0) - onehot
    ranking = jnp.sum(before * onehot, axis=1)
    position = owners * capacity + ranking
    wanted = (
        jnp.zeros((axis_rows * capacity,), jnp.int32).at[position].set(columns_flat % per_owner)
    )
    return (position, wanted.reshape(axis_rows, capacity))


def send_back(wanted, local_blocks):
    blocks = local_blocks[wanted]
    return lax.all_to_all(blocks, "rows", split_axis=0, concat_axis=0, tiled=True)


def row_products(values_rows, positions_rows, counts_rows, table):
    slot_count = values_rows.shape[1]
    slot_ids = jnp.arange(slot_count, dtype=jnp.int32)

    def one_row(entries):
        values_row, positions_row, counts_row = entries
        picked = table[positions_row]
        live_mask = (slot_ids < counts_row[0]).astype(jnp.bfloat16)
        picked = picked * live_mask[:, None, None]
        return jnp.einsum("sab,sbk->ak", values_row, picked, preferred_element_type=jnp.float32)

    result = lax.map(one_row, (values_rows, positions_rows, counts_rows))
    return result.reshape(-1, table.shape[2])


def per_device(block_values, block_columns, row_counts, sketch):
    block_order = block_values.shape[2]
    sketch_width = sketch.shape[1]
    axis_rows = lax.axis_size("rows")
    slot_total = block_columns.shape[0] * block_columns.shape[1]
    capacity = 3 * slot_total // (2 * axis_rows)
    local_blocks = sketch.reshape(-1, block_order, sketch_width)
    per_owner = local_blocks.shape[0]
    position, wanted_here = request_table(block_columns.reshape(-1), per_owner, axis_rows, capacity)
    table = send_back(
        lax.all_to_all(wanted_here, "rows", split_axis=0, concat_axis=0, tiled=True), local_blocks
    )
    table = table.reshape(-1, block_order, sketch_width)
    positions = position.reshape(block_columns.shape[0], block_columns.shape[1])
    partial_image = row_products(block_values, positions, row_counts, table)
    image_here = lax.psum_scatter(partial_image, "cols", scatter_dimension=0, tiled=True)
    total_rows = image_here.shape[0] * lax.axis_size("rows") * lax.axis_size("cols")
    gram_local = jnp.dot(
        image_here.T,
        image_here,
        precision=lax.Precision.HIGHEST,
        preferred_element_type=jnp.float32,
    )
    gram_matrix = lax.psum(gram_local, ("rows", "cols")) / total_rows
    lower_factor = jnp.linalg.cholesky(gram_matrix)
    basis_rows = jax.scipy.linalg.solve_triangular(lower_factor, image_here.T, lower=True).T
    return (basis_rows, lower_factor.T)


def solution(mesh):
    return jax.shard_map(
        per_device,
        mesh=mesh,
        in_specs=(
            P("rows", "cols", None, None),
            P("rows", "cols"),
            P("rows", "cols"),
            P(("rows", "cols"), None),
        ),
        out_specs=(P(("rows", "cols"), None), P()),
        check_vma=False,
    )
```

profile of v0, /device:TPU:2, one launch (start us, length us, event | category | flops | bytes accessed | tf_op | source)
XLA Modules:
  0.0 1127.3 jit_solution(16945406172135663035)
XLA Ops:
  10.6 1.4 scatter_custom_fusion
  12.1 20.0 %all_to_all.17 = s32[32,1,12]{2,1,0:T(1,128)S(1)} all-to-all(s32[32,1,12]{2,1,0:T(1,128)S(1)} %bitcast.99), channel_id=1, replica_groups=mesh['rows'=32,'cols'=8] {'rows'}, dimensions={0} | all-to-all | bytes 3072 | tf_op jit(solution)/shard_map/all_to_all | solution.py:49
  32.2 12.9 %gather_fusion.1 = bf16[384,128,256]{2,1,0:T(8,128)(2,1)} fusion(bf16[32,128,256]{2,1,0:T(8,128)(2,1)S(1)} %bitcast.94, s32[1024]{0:T(1024)S(1)} %pad_clamp_fusion.1), kind=kCustom, calls=%fused_computation.1 | custom fusion | bytes 50333184 | tf_op jit(solution)/shard_map/gather | solution.py:20
  45.1 6.5 all-to-all-start.1
  51.7 577.4 %all-to-all-done.1 = bf16[32,12,128,256]{3,2,1,0:T(8,128)(2,1)} async-done(((bf16[32,12,128,256]{3,2,1,0:T(8,128)(2,1)}), bf16[32,12,128,256]{3,2,1,0:T(8,128)(2,1)}, u32[]{:S(2)}, u32[]{:S(2)}) %all-to-all-start.1) | async-done | bytes 25165856 | tf_op jit(solution)/shard_map/all_to_all | solution.py:21
  629.1 95.0 %while.13 = (s32[]{:T(128)}, f32[8,128,256]{2,1,0:T(8,128)S(1)}, bf16[8,32,128,128]{3,2,1,0:T(8,128)(2,1)}, s32[8,32]{1,0:T(8,128)S(1)}, bf16[384,128,256]{2,1,0:T(8,128)(2,1)}, /*index=5*/s32[8,1]{0,1:T(1,128)S(1)}, s32[]{:T(128)}) while((s32[]{:T(128)}, f32[8,128,256]{2,1,0:T(8,128)S(1)}, bf16[8,32,128,128]{3,2,1,0:T(8,128)(2,1)}, ...), condition=%wide.region_5.6_spmd.clone, body=%wide.region_4.5_spmd.clone.sunk | while | flops 269485216 | bytes 7477409 | solution.py:35
  629.1 8.8 gather_fusion
  639.2 1.8 fusion.53
  641.0 8.8 gather_fusion
  651.1 1.8 fusion.53
  652.9 8.8 gather_fusion
  663.0 1.8 fusion.53
  664.8 8.8 gather_fusion
  674.8 1.8 fusion.53
  676.6 8.8 gather_fusion
  686.7 1.8 fusion.53
  688.5 8.8 gather_fusion
  698.6 1.8 fusion.53
  700.4 8.8 gather_fusion
  710.5 1.8 fusion.53
  712.3 8.8 gather_fusion
  722.4 1.8 fusion.53
  725.7 70.9 %reduce-scatter.2.cloned.1.call-done = f32[128,256]{0,1:T(8,128)} async-done(((f32[1024,256]{0,1:T(8,128)}), f32[128,256]{0,1:T(8,128)}) %reduce-scatter.2.cloned.1.call-update) | async-done | bytes 131088 | tf_op jit(solution)/shard_map/reduce_scatter | solution.py:54
  796.6 2.1 fusion.37
  798.7 257.2 %all-reduce.3.cloned.1.call-done = f32[256,256]{0,1:T(8,128)} async-done(((f32[256,256]{0,1:T(8,128)}), f32[256,256]{0,1:T(8,128)}) %all-reduce.3.cloned.1.call-update) | async-done | bytes 262160 | tf_op jit(solution)/shard_map/psum | solution.py:62
  1058.0 11.7 %cholesky.50 = f32[128,128]{1,0:T(8,128)S(1)} custom-call(f32[128,128]{1,0:T(8,128)S(1)} %cholesky.118), custom_call_target="Cholesky" | custom-call | tf_op jit(solution)/shard_map/jit(cholesky)/cholesky | solution.py:63
  1069.8 9.8 custom-call.15
  1080.1 11.7 %cholesky.105 = f32[128,128]{1,0:T(8,128)S(1)} custom-call(f32[128,128]{1,0:T(8,128)S(1)} %convolution_subtract_fusion.1), custom_call_target="Cholesky" | custom-call | tf_op jit(solution)/shard_map/jit(cholesky)/cholesky | solution.py:63
  1094.0 4.3 while.12
  1094.8 1.4 bitcast_dynamic-update-slice_fusion.2
  1096.9 1.4 bitcast_dynamic-update-slice_fusion.2
  1098.3 19.7 %custom-call.16 = f32[2,128,128]{1,2,0:T(8,128)S(1)} custom-call(f32[2,128,128]{2,1,0:T(8,128)S(1)} %get-tuple-element.47), custom_call_target="InvertDiagBlocksLowerTriangular" | custom-call | tf_op jit(solution)/shard_map/jit(_solve_triangular)/triangular_solve | solution.py:64
  (90 shorter events, 22.3 us)
Async XLA Ops:
  7.2 25.0 %copy-start = (bf16[4096,256]{1,0:T(8,128)(2,1)S(1)}, bf16[4096,256]{1,0:T(8,128)(2,1)}, u32[]{:S(2)}) copy-start(bf16[4096,256]{1,0:T(8,128)(2,1)} %param.9) | copy-start | bytes 6291460
  45.1 6.6 copy-start.3
  45.1 584.0 %copy-start.4 = (s32[8,1]{0,1:T(1,128)S(1)}, s32[8,1]{0,1:T(1,128)}, u32[]{:S(2)}) copy-start(s32[8,1]{0,1:T(1,128)} %param.8) | copy-start | bytes 100
  45.1 584.0 %all-to-all-start.1 = ((bf16[32,12,128,256]{3,2,1,0:T(8,128)(2,1)}), bf16[32,12,128,256]{3,2,1,0:T(8,128)(2,1)}, u32[]{:S(2)}, u32[]{:S(2)}) async-start(bf16[32,12,128,256]{3,2,1,0:T(8,128)(2,1)} %bitcast.95), calls=%async_computation.1 | async-start | bytes 50331648 | tf_op jit(solution)/shard_map/all_to_all | solution.py:21
  51.6 745.0 %reduce-scatter.2.cloned.1.call-start = ((), (), s32[]{:S(2)}) async-start(), calls=%async_computation.3 | async-start | bytes 1179648 | tf_op jit(solution)/shard_map/reduce_scatter | solution.py:54
  725.5 330.4 %all-reduce.3.cloned.1.call-start = ((), (), s32[]{:S(2)}) async-start(), calls=%async_computation.4 | async-start | bytes 524288 | tf_op jit(solution)/shard_map/psum | solution.py:62
  1056.9 61.1 %copy-start.2 = (f32[128,256]{0,1:T(8,128)S(1)}, f32[128,256]{0,1:T(8,128)}, u32[]{:S(2)}) copy-start(f32[128,256]{0,1:T(8,128)} %reduce-scatter.2.cloned.1.call-done) | copy-start | bytes 393220
  1069.8 50.6 %copy-start.1 = (bf16[4096,256]{1,0:T(8,128)(2,1)S(1)}, bf16[4096,256]{1,0:T(8,128)(2,1)}, u32[]{:S(2)}) copy-start(bf16[4096,256]{1,0:T(8,128)(2,1)} %param.9) | copy-start | bytes 6291460
Sparse Core Ops, SparseCore 0:
  725.6 70.9 reduce-scatter.1
  802.6 253.2 all-reduce.2
where the time goes:
time: 1130 us
  waiting for transfers between devices  905 us (80%)
  local copies, waits for them, and re-layouts  99.9 us (9%)
  other arithmetic  61.6 us (5%)
  blocking collectives  20 us (2%)
  matrix products  17.3 us (2%)
  between operations  15.6 us (1%)
    all_to_all x1, waiting for transfers between devices, send_back(): lax.all_to_all(blocks, 'rows', split_axis=0, concat_axis=0, tiled=True)  577 us
    psum x1, waiting for transfers between devices, per_device(): gram_matrix = lax.psum(gram_local, ('rows', 'cols')) / total_rows  257 us
    reduce_scatter x1, waiting for transfers between devices, per_device(): lax.psum_scatter(partial_image, 'cols', scatter_dimension=0, tiled=True)  70.9 us
    gather x8, local copies, waits for them, and re-layouts, one_row(): picked = table[positions_row]  70.7 us
    another operation x6, other arithmetic, per_device(): lower_factor = jnp.linalg.cholesky(gram_matrix)  34 us
  transfers between devices with their start and end apart: 3, of which 3 were waited for; matrix products, arithmetic and copies ran while one was open for 0% of the time, Pallas kernels for 0%

commit v1 on v0

--- a/solution.py
+++ b/solution.py
@@ -59,7 +59,9 @@
         precision=lax.Precision.HIGHEST,
         preferred_element_type=jnp.float32,
     )
-    gram_matrix = lax.psum(gram_local, ("rows", "cols")) / total_rows
+    gram_matrix = (
+        jax.lax.psum(jax.lax.psum(gram_local, axis_name="cols"), axis_name="rows") / total_rows
+    )
     lower_factor = jnp.linalg.cholesky(gram_matrix)
     basis_rows = jax.scipy.linalg.solve_triangular(lower_factor, image_here.T, lower=True).T
     return (basis_rows, lower_factor.T)

time: 1130 us -> 1080 us (0.956)
  waiting for transfers between devices: 905 us -> 860 us
    psum x1 -> x2, waiting for transfers between devices: 257 us -> 212 us  [the longest x1 147 us: per_device(): jax.lax.psum(jax.lax.psum(gram_local, axis_name='cols'), axis_name='rows')]
  transfers between devices with their start and end apart: 3 -> 4, of which waited for: 3 -> 4; matrix products, arithmetic and copies ran while one was open for 0% -> 0% of each run, Pallas kernels for 0% -> 0%
where the time goes in v1:
time: 1080 us
  waiting for transfers between devices  860 us (80%)
  local copies, waits for them, and re-layouts  99.9 us (9%)
  other arithmetic  61.6 us (6%)
  blocking collectives  20 us (2%)
  matrix products  17.3 us (2%)
  between operations  15.3 us (1%)
    all_to_all x1, waiting for transfers between devices, send_back(): lax.all_to_all(blocks, 'rows', split_axis=0, concat_axis=0, tiled=True)  577 us
    psum x1, waiting for transfers between devices, per_device(): jax.lax.psum(jax.lax.psum(gram_local, axis_name='cols'), axis_name='rows')  147 us
    reduce_scatter x1, waiting for transfers between devices, per_device(): lax.psum_scatter(partial_image, 'cols', scatter_dimension=0, tiled=True)  71.1 us
    gather x8, local copies, waits for them, and re-layouts, one_row(): picked = table[positions_row]  70.7 us
    psum x1, waiting for transfers between devices, per_device(): jax.lax.psum(gram_local, axis_name='cols')  65 us
    another operation x6, other arithmetic, per_device(): lower_factor = jnp.linalg.cholesky(gram_matrix)  34 us
  transfers between devices with their start and end apart: 4, of which 4 were waited for; matrix products, arithmetic and copies ran while one was open for 0% of the time, Pallas kernels for 0%

profile of v1, /device:TPU:2, one launch (start us, length us, event | category | flops | bytes accessed | tf_op | source)
XLA Modules:
  0.0 1081.9 jit_solution(9314899777730781380)
XLA Ops:
  12.1 20.0 %all_to_all.17 = s32[32,1,12]{2,1,0:T(1,128)S(1)} all-to-all(s32[32,1,12]{2,1,0:T(1,128)S(1)} %bitcast.99), channel_id=1, replica_groups=mesh['rows'=32,'cols'=8] {'rows'}, dimensions={0} | all-to-all | bytes 3072 | tf_op jit(solution)/shard_map/all_to_all | solution.py:49
  32.2 12.9 %gather_fusion.1 = bf16[384,128,256]{2,1,0:T(8,128)(2,1)} fusion(bf16[32,128,256]{2,1,0:T(8,128)(2,1)S(1)} %bitcast.94, s32[1024]{0:T(1024)S(1)} %pad_clamp_fusion.1), kind=kCustom, calls=%fused_computation.1 | custom fusion | bytes 50333184 | tf_op jit(solution)/shard_map/gather | solution.py:20
  45.1 6.5 all-to-all-start.1
  51.7 577.4 %all-to-all-done.1 = bf16[32,12,128,256]{3,2,1,0:T(8,128)(2,1)} async-done(((bf16[32,12,128,256]{3,2,1,0:T(8,128)(2,1)}), bf16[32,12,128,256]{3,2,1,0:T(8,128)(2,1)}, u32[]{:S(2)}, u32[]{:S(2)}) %all-to-all-start.1) | async-done | bytes 25165856 | tf_op jit(solution)/shard_map/all_to_all | solution.py:21
  629.1 95.0 %while.13 = (s32[]{:T(128)}, f32[8,128,256]{2,1,0:T(8,128)S(1)}, bf16[8,32,128,128]{3,2,1,0:T(8,128)(2,1)}, s32[8,32]{1,0:T(8,128)S(1)}, bf16[384,128,256]{2,1,0:T(8,128)(2,1)}, /*index=5*/s32[8,1]{0,1:T(1,128)S(1)}, s32[]{:T(128)}) while((s32[]{:T(128)}, f32[8,128,256]{2,1,0:T(8,128)S(1)}, bf16[8,32,128,128]{3,2,1,0:T(8,128)(2,1)}, ...), condition=%wide.region_5.6_spmd.clone, body=%wide.region_4.5_spmd.clone.sunk | while | flops 269485216 | bytes 7477409 | solution.py:35
  629.1 8.8 gather_fusion
  639.2 1.8 fusion.53
  641.0 8.8 gather_fusion
  651.1 1.8 fusion.53
  652.9 8.8 gather_fusion
  663.0 1.8 fusion.53
  664.8 8.8 gather_fusion
  674.8 1.8 fusion.53
  676.6 8.8 gather_fusion
  686.7 1.8 fusion.53
  688.5 8.8 gather_fusion
  698.6 1.8 fusion.53
  700.4 8.8 gather_fusion
  710.5 1.8 fusion.53
  712.3 8.8 gather_fusion
  722.4 1.8 fusion.53
  725.5 71.1 %reduce-scatter.2.cloned.1.call-done = f32[128,256]{0,1:T(8,128)} async-done(((f32[1024,256]{0,1:T(8,128)}), f32[128,256]{0,1:T(8,128)}) %reduce-scatter.2.cloned.1.call-update) | async-done | bytes 131088 | tf_op jit(solution)/shard_map/reduce_scatter | solution.py:54
  796.6 2.1 fusion.37
  798.9 65.0 %all-reduce.4.cloned.1.call-done = f32[256,256]{0,1:T(8,128)} async-done(((f32[256,256]{0,1:T(8,128)}), f32[256,256]{0,1:T(8,128)}) %all-reduce.4.cloned.1.call-update) | async-done | bytes 262160 | tf_op jit(solution)/shard_map/psum | solution.py:63
  863.9 146.9 %all-reduce.6.cloned.1.call-done = f32[256,256]{0,1:T(8,128)} async-done(((f32[256,256]{0,1:T(8,128)}), f32[256,256]{0,1:T(8,128)}) %all-reduce.6.cloned.1.call-update) | async-done | bytes 262160 | tf_op jit(solution)/shard_map/psum | solution.py:63
  1013.0 11.7 %cholesky.50 = f32[128,128]{1,0:T(8,128)S(1)} custom-call(f32[128,128]{1,0:T(8,128)S(1)} %cholesky.118), custom_call_target="Cholesky" | custom-call | tf_op jit(solution)/shard_map/jit(cholesky)/cholesky | solution.py:65
  1024.7 9.8 custom-call.15
  1035.0 11.7 %cholesky.105 = f32[128,128]{1,0:T(8,128)S(1)} custom-call(f32[128,128]{1,0:T(8,128)S(1)} %convolution_subtract_fusion.1), custom_call_target="Cholesky" | custom-call | tf_op jit(solution)/shard_map/jit(cholesky)/cholesky | solution.py:65
  1049.0 4.3 while.12
  1049.8 1.4 bitcast_dynamic-update-slice_fusion.2
  1051.8 1.4 bitcast_dynamic-update-slice_fusion.2
  1053.3 19.7 %custom-call.16 = f32[2,128,128]{1,2,0:T(8,128)S(1)} custom-call(f32[2,128,128]{2,1,0:T(8,128)S(1)} %get-tuple-element.47), custom_call_target="InvertDiagBlocksLowerTriangular" | custom-call | tf_op jit(solution)/shard_map/jit(_solve_triangular)/triangular_solve | solution.py:66
  (93 shorter events, 23.8 us)
Async XLA Ops:
  7.2 25.0 %copy-start = (bf16[4096,256]{1,0:T(8,128)(2,1)S(1)}, bf16[4096,256]{1,0:T(8,128)(2,1)}, u32[]{:S(2)}) copy-start(bf16[4096,256]{1,0:T(8,128)(2,1)} %param.9) | copy-start | bytes 6291460
  45.1 6.6 copy-start.3
  45.1 584.0 %copy-start.4 = (s32[8,1]{0,1:T(1,128)S(1)}, s32[8,1]{0,1:T(1,128)}, u32[]{:S(2)}) copy-start(s32[8,1]{0,1:T(1,128)} %param.8) | copy-start | bytes 100
  45.1 584.0 %all-to-all-start.1 = ((bf16[32,12,128,256]{3,2,1,0:T(8,128)(2,1)}), bf16[32,12,128,256]{3,2,1,0:T(8,128)(2,1)}, u32[]{:S(2)}, u32[]{:S(2)}) async-start(bf16[32,12,128,256]{3,2,1,0:T(8,128)(2,1)} %bitcast.95), calls=%async_computation.1 | async-start | bytes 50331648 | tf_op jit(solution)/shard_map/all_to_all | solution.py:21
  51.6 745.0 %reduce-scatter.2.cloned.1.call-start = ((), (), s32[]{:S(2)}) async-start(), calls=%async_computation.3 | async-start | bytes 1179648 | tf_op jit(solution)/shard_map/reduce_scatter | solution.py:54
  725.5 138.4 %all-reduce.4.cloned.1.call-start = ((), (), s32[]{:S(2)}) async-start(), calls=%async_computation.4 | async-start | bytes 524288 | tf_op jit(solution)/shard_map/psum | solution.py:63
  798.7 212.2 %all-reduce.6.cloned.1.call-start = ((), (), s32[]{:S(2)}) async-start(), calls=%async_computation.5 | async-start | bytes 524288 | tf_op jit(solution)/shard_map/psum | solution.py:63
  1011.8 61.1 %copy-start.2 = (f32[128,256]{0,1:T(8,128)S(1)}, f32[128,256]{0,1:T(8,128)}, u32[]{:S(2)}) copy-start(f32[128,256]{0,1:T(8,128)} %reduce-scatter.2.cloned.1.call-done) | copy-start | bytes 393220
  1024.7 50.6 %copy-start.1 = (bf16[4096,256]{1,0:T(8,128)(2,1)S(1)}, bf16[4096,256]{1,0:T(8,128)(2,1)}, u32[]{:S(2)}) copy-start(bf16[4096,256]{1,0:T(8,128)(2,1)} %param.9) | copy-start | bytes 6291460
Sparse Core Ops, SparseCore 0:
  725.6 70.9 reduce-scatter.1
  799.5 64.3 all-reduce.3
  867.3 143.4 all-reduce.5
